TPU v7x, 32 devices: a whole 2x2x4 slice. The times are simulated.
32 devices in a mesh: shard: 8 (over y, x, core), rep: 4 (over z).
Axes of the slice: x: 2, y: 2, z: 4, core: 2. Of those that a mesh axis runs over, the one named last changes fastest.
Arguments:
- tokens: bfloat16 [2, 16384, 768], P(None, ('shard', 'rep')), may hold values from -6 to 6
- segment_ids: int32 [2, 16384], P(None, ('shard', 'rep')), may hold values from 0 to 7, as said below
- qkv_weight: bfloat16 [768, 2304], P('shard'), may hold values from -0.21875 to 0.21875
- out_weight: bfloat16 [768, 768], P('shard'), may hold values from -0.875 to 0.875
- gate_weight: bfloat16 [768, 3072], P('shard'), may hold values from -0.21875 to 0.21875
- up_weight: bfloat16 [768, 3072], P('shard'), may hold values from -0.21875 to 0.21875
- down_weight: bfloat16 [3072, 768], P('shard'), may hold values from -0.109375 to 0.109375
- norm1_gain: bfloat16 [768], P('shard'), may hold values from 0.5 to 1.5
- norm1_bias: bfloat16 [768], P('shard'), may hold values from -1 to 1
- norm2_gain: bfloat16 [768], P('shard'), may hold values from 0.5 to 1.5
- norm2_bias: bfloat16 [768], P('shard'), may hold values from -1 to 1
- out_grad: bfloat16 [2, 16384, 768], P(None, ('shard', 'rep')), may hold values from -6 to 6
Outputs:
- output: bfloat16 [2, 16384, 768], P(None, ('shard', 'rep'))
- input_grad: bfloat16 [2, 16384, 768], P(None, ('shard', 'rep'))
- qkv_weight_grad: float32 [768, 2304], P('shard')
- out_weight_grad: float32 [768, 768], P('shard')
- gate_weight_grad: float32 [768, 3072], P('shard')
- up_weight_grad: float32 [768, 3072], P('shard')
- down_weight_grad: float32 [3072, 768], P('shard')
- norm1_gain_grad: float32 [768], P('shard')
- norm1_bias_grad: float32 [768], P('shard')
- norm2_gain_grad: float32 [768], P('shard')
- norm2_bias_grad: float32 [768], P('shard')
Inputs may be any that keep to these rules, and one draw needn't show every extreme that they name: Within each packed sequence of 512 tokens segment_ids never falls, starts at 0, and takes each value 0 to 7 on a run of one or more tokens.
All inputs are finite; a program needn't handle non-finite values.
Results may differ from a plain program's by a relative error of at most 0.02.
Values may be sent and summed in bfloat16 or wider, within the bound.
No kernel may reach another device: no remote copies, remote signals or barrier semaphores. Data moves between devices by JAX's collectives and lax.ppermute only.
A program may use at most 192 MiB of HBM per device.

v0:
```python
import jax
import jax.numpy as jnp
from jax import lax
from jax.sharding import PartitionSpec as P

HEAD_DIM = 64
norm_eps = 1e-12
rope_base = 1000.0
masked_score = -1000000000.0


def matmul(left_op, right_op):
    return jnp.dot(left_op, right_op, preferred_element_type=jnp.float32)


def inner_sum(left_op, right_op):
    return lax.dot_general(
        left_op, right_op, (((0,), (0,)), ((), ())), preferred_element_type=jnp.float32
    )


def times_transposed(left_op, right_op):
    return lax.dot_general(
        left_op, right_op, (((1,), (1,)), ((), ())), preferred_element_type=jnp.float32
    )


def rope_tables(seq_len, head_dim):
    places = jnp.arange(seq_len, dtype=jnp.int32).astype(jnp.float32)
    frequency = rope_base ** (-jnp.arange(0, head_dim, 2, dtype=jnp.float32) / head_dim)
    angles = places[:, None] * frequency[None, :]
    cos_table = jnp.cos(angles)
    sin_table = jnp.sin(angles)
    return (
        jnp.concatenate([cos_table, cos_table], -1),
        jnp.concatenate([sin_table, sin_table], -1),
    )


def rotate(values, cos_table, sin_table):
    half_dim = values.shape[-1] // 2
    turned = jnp.concatenate([-values[..., half_dim:], values[..., :half_dim]], -1)
    return values * cos_table + turned * sin_table


def rotate_back(grad_in, cos_table, sin_table):
    half_dim = grad_in.shape[-1] // 2
    scaled = grad_in * sin_table
    turned = jnp.concatenate([scaled[..., half_dim:], -scaled[..., :half_dim]], -1)
    return grad_in * cos_table + turned


def normalize(hidden_in):
    centre = hidden_in - jnp.mean(hidden_in, -1, keepdims=True)
    inv_std = lax.rsqrt(jnp.mean(centre * centre, -1, keepdims=True) + norm_eps)
    return (centre * inv_std, inv_std)


def norm_back(grad_norm, normed, inv_std):
    return inv_std * (
        grad_norm
        - jnp.mean(grad_norm, -1, keepdims=True)
        - normed * jnp.mean(grad_norm * normed, -1, keepdims=True)
    )


def attend_head(query_h, key_h, value_h, same_doc):
    scores = jnp.where(same_doc, times_transposed(query_h, key_h) * 0.125, masked_score)
    row_max = jnp.max(scores, -1, keepdims=True)
    expo = jnp.exp(scores - row_max)
    total_sum = jnp.sum(expo, -1, keepdims=True)
    probs = expo / total_sum
    result = matmul(probs.astype(jnp.bfloat16), value_h)
    return (result, (row_max + jnp.log(total_sum))[:, 0])


def head_backward(query_h, key_h, value_h, grad_h, log_total, same_doc):
    scores = jnp.where(same_doc, times_transposed(query_h, key_h) * 0.125, masked_score)
    probs = jnp.exp(scores - log_total[:, None])
    grad_value = inner_sum(probs.astype(jnp.bfloat16), grad_h)
    grad_probs = times_transposed(grad_h, value_h)
    grad_scores = (probs * (grad_probs - jnp.sum(probs * grad_probs, -1, keepdims=True))).astype(
        jnp.bfloat16
    )
    grad_query = matmul(grad_scores, key_h) * 0.125
    grad_key = inner_sum(grad_scores, query_h) * 0.125
    return (grad_query, grad_key, grad_value)


def forward_pass(token_rows, segment, weight_set):
    full_qkv, full_out, full_gate, full_up, full_down, gain_one, bias_one, gain_two, bias_two = (
        weight_set
    )
    seq_len = token_rows.shape[0]
    width = full_out.shape[0]
    head_count = width // HEAD_DIM
    cos_table, sin_table = rope_tables(seq_len, HEAD_DIM)
    cos_heads = cos_table[:, None, :]
    sin_heads = sin_table[:, None, :]
    joint = matmul(token_rows, full_qkv)
    queries = (
        rotate(joint[:, :width].reshape(seq_len, head_count, HEAD_DIM), cos_heads, sin_heads)
        .astype(jnp.bfloat16)
        .transpose(1, 0, 2)
    )
    key_rows = (
        rotate(
            joint[:, width : 2 * width].reshape(seq_len, head_count, HEAD_DIM), cos_heads, sin_heads
        )
        .astype(jnp.bfloat16)
        .transpose(1, 0, 2)
    )
    value_rows = (
        joint[:, 2 * width :]
        .reshape(seq_len, head_count, HEAD_DIM)
        .astype(jnp.bfloat16)
        .transpose(1, 0, 2)
    )
    same_doc = segment[:, None] == segment[None, :]
    attended, log_total = lax.map(
        lambda operands: attend_head(operands[0], operands[1], operands[2], same_doc),
        (queries, key_rows, value_rows),
    )
    attended_low = attended.transpose(1, 0, 2).reshape(seq_len, width).astype(jnp.bfloat16)
    residual_one = token_rows.astype(jnp.float32) + matmul(attended_low, full_out)
    normed_one, inv_one = normalize(residual_one)
    mixed = normed_one * gain_one.astype(jnp.float32) + bias_one.astype(jnp.float32)
    mixed_low = mixed.astype(jnp.bfloat16)
    gate_pre = matmul(mixed_low, full_gate)
    up_pre = matmul(mixed_low, full_up)
    sigmoid_gate = jax.nn.sigmoid(gate_pre)
    hidden_low = (gate_pre * sigmoid_gate * up_pre).astype(jnp.bfloat16)
    residual_two = mixed + matmul(hidden_low, full_down)
    normed_two, inv_two = normalize(residual_two)
    layer_out = (normed_two * gain_two.astype(jnp.float32) + bias_two.astype(jnp.float32)).astype(
        jnp.bfloat16
    )
    kept = {
        "token_rows": token_rows,
        "cos_heads": cos_heads,
        "sin_heads": sin_heads,
        "queries": queries,
        "key_rows": key_rows,
        "value_rows": value_rows,
        "log_total": log_total,
        "same_doc": same_doc,
        "attended_low": attended_low,
        "normed_one": normed_one,
        "inv_one": inv_one,
        "mixed_low": mixed_low,
        "gate_pre": gate_pre,
        "up_pre": up_pre,
        "sigmoid_gate": sigmoid_gate,
        "hidden_low": hidden_low,
        "normed_two": normed_two,
        "inv_two": inv_two,
    }
    return (kept, layer_out)


def backward_pass(kept, weight_set, cotangent):
    full_qkv, full_out, full_gate, full_up, full_down, gain_one, gain_two = weight_set
    token_rows = kept["token_rows"]
    seq_len = token_rows.shape[0]
    width = full_out.shape[0]
    head_count = width // HEAD_DIM
    grad_gain_two = jnp.sum(cotangent * kept["normed_two"], 0)
    grad_bias_two = jnp.sum(cotangent, 0)
    grad_res_two = norm_back(
        cotangent * gain_two.astype(jnp.float32), kept["normed_two"], kept["inv_two"]
    )
    grad_mlp = grad_res_two.astype(jnp.bfloat16)
    grad_down = inner_sum(kept["hidden_low"], grad_mlp)
    grad_hidden = times_transposed(grad_mlp, full_down)
    gate_pre = kept["gate_pre"]
    sigmoid_gate = kept["sigmoid_gate"]
    grad_up_pre = (grad_hidden * gate_pre * sigmoid_gate).astype(jnp.bfloat16)
    grad_gate_pre = (
        grad_hidden * kept["up_pre"] * sigmoid_gate * (1.0 + gate_pre * (1.0 - sigmoid_gate))
    ).astype(jnp.bfloat16)
    grad_gate = inner_sum(kept["mixed_low"], grad_gate_pre)
    grad_up = inner_sum(kept["mixed_low"], grad_up_pre)
    grad_mixed = (
        grad_res_two
        + times_transposed(grad_gate_pre, full_gate)
        + times_transposed(grad_up_pre, full_up)
    )
    grad_gain_one = jnp.sum(grad_mixed * kept["normed_one"], 0)
    grad_bias_one = jnp.sum(grad_mixed, 0)
    grad_res_one = norm_back(
        grad_mixed * gain_one.astype(jnp.float32), kept["normed_one"], kept["inv_one"]
    )
    grad_branch = grad_res_one.astype(jnp.bfloat16)
    grad_out = inner_sum(kept["attended_low"], grad_branch)
    grad_att = (
        times_transposed(grad_branch, full_out)
        .astype(jnp.bfloat16)
        .reshape(seq_len, head_count, HEAD_DIM)
        .transpose(1, 0, 2)
    )
    same_doc = kept["same_doc"]
    grad_query, grad_key, grad_value = lax.map(
        lambda operands: head_backward(
            operands[0], operands[1], operands[2], operands[3], operands[4], same_doc
        ),
        (kept["queries"], kept["key_rows"], kept["value_rows"], grad_att, kept["log_total"]),
    )
    query_part = rotate_back(
        grad_query.transpose(1, 0, 2), kept["cos_heads"], kept["sin_heads"]
    ).reshape(seq_len, width)
    key_part = rotate_back(
        grad_key.transpose(1, 0, 2), kept["cos_heads"], kept["sin_heads"]
    ).reshape(seq_len, width)
    value_part = grad_value.transpose(1, 0, 2).reshape(seq_len, width)
    grad_joint = jnp.concatenate([query_part, key_part, value_part], -1).astype(jnp.bfloat16)
    grad_qkv = inner_sum(token_rows, grad_joint)
    input_grad = (grad_res_one + times_transposed(grad_joint, full_qkv)).astype(jnp.bfloat16)
    return (
        (
            grad_qkv,
            grad_out,
            grad_gate,
            grad_up,
            grad_down,
            grad_gain_one,
            grad_bias_one,
            grad_gain_two,
            grad_bias_two,
        ),
        input_grad,
    )


def shards(
    tokens,
    segment_ids,
    qkv_weight,
    out_weight,
    gate_weight,
    up_weight,
    down_weight,
    norm1_gain,
    norm1_bias,
    norm2_gain,
    norm2_bias,
    out_grad,
):
    owned_shards = (
        qkv_weight,
        out_weight,
        gate_weight,
        up_weight,
        down_weight,
        norm1_gain,
        norm1_bias,
        norm2_gain,
        norm2_bias,
    )
    group_count = lax.axis_size("shard")
    summed = tuple(
        (
            jnp.zeros((weight_piece.shape[0] * group_count,) + weight_piece.shape[1:], jnp.float32)
            for weight_piece in owned_shards
        )
    )
    outputs = []
    input_grads = []
    for micro_step in range(tokens.shape[0]):
        forward_set = (
            lax.all_gather(qkv_weight, "shard", axis=0, tiled=True),
            lax.all_gather(out_weight, "shard", axis=0, tiled=True),
            lax.all_gather(gate_weight, "shard", axis=0, tiled=True),
            lax.all_gather(up_weight, "shard", axis=0, tiled=True),
            lax.all_gather(down_weight, "shard", axis=0, tiled=True),
            lax.all_gather(norm1_gain, "shard", axis=0, tiled=True),
            lax.all_gather(norm1_bias, "shard", axis=0, tiled=True),
            lax.all_gather(norm2_gain, "shard", axis=0, tiled=True),
            lax.all_gather(norm2_bias, "shard", axis=0, tiled=True),
        )
        kept, layer_out = forward_pass(tokens[micro_step], segment_ids[micro_step], forward_set)
        backward_set = (
            lax.all_gather(qkv_weight, "shard", axis=0, tiled=True),
            lax.all_gather(out_weight, "shard", axis=0, tiled=True),
            lax.all_gather(gate_weight, "shard", axis=0, tiled=True),
            lax.all_gather(up_weight, "shard", axis=0, tiled=True),
            lax.all_gather(down_weight, "shard", axis=0, tiled=True),
            lax.all_gather(norm1_gain, "shard", axis=0, tiled=True),
            lax.all_gather(norm2_gain, "shard", axis=0, tiled=True),
        )
        grad_set, input_grad = backward_pass(
            kept, backward_set, out_grad[micro_step].astype(jnp.float32)
        )
        outputs.append(layer_out)
        input_grads.append(input_grad)
        summed = tuple((left_sum + right_sum for left_sum, right_sum in zip(summed, grad_set)))
    (
        sum_qkv,
        sum_out,
        sum_gate,
        sum_up,
        sum_down,
        sum_gain_one,
        sum_bias_one,
        sum_gain_two,
        sum_bias_two,
    ) = summed
    summed = (
        lax.psum_scatter(
            sum_qkv.astype(jnp.bfloat16), "shard", scatter_dimension=0, tiled=True
        ).astype(jnp.float32),
        lax.psum_scatter(
            sum_out.astype(jnp.bfloat16), "shard", scatter_dimension=0, tiled=True
        ).astype(jnp.float32),
        lax.psum_scatter(
            sum_gate.astype(jnp.bfloat16), "shard", scatter_dimension=0, tiled=True
        ).astype(jnp.float32),
        lax.psum_scatter(
            sum_up.astype(jnp.bfloat16), "shard", scatter_dimension=0, tiled=True
        ).astype(jnp.float32),
        lax.psum_scatter(
            sum_down.astype(jnp.bfloat16), "shard", scatter_dimension=0, tiled=True
        ).astype(jnp.float32),
        lax.psum_scatter(
            sum_gain_one.astype(jnp.bfloat16), "shard", scatter_dimension=0, tiled=True
        ).astype(jnp.float32),
        lax.psum_scatter(
            sum_bias_one.astype(jnp.bfloat16), "shard", scatter_dimension=0, tiled=True
        ).astype(jnp.float32),
        lax.psum_scatter(
            sum_gain_two.astype(jnp.bfloat16), "shard", scatter_dimension=0, tiled=True
        ).astype(jnp.float32),
        lax.psum_scatter(
            sum_bias_two.astype(jnp.bfloat16), "shard", scatter_dimension=0, tiled=True
        ).astype(jnp.float32),
    )
    (
        part_qkv,
        part_out,
        part_gate,
        part_up,
        part_down,
        part_gain_one,
        part_bias_one,
        part_gain_two,
        part_bias_two,
    ) = summed
    totals = (
        lax.psum(part_qkv.astype(jnp.bfloat16), "rep").astype(jnp.float32),
        lax.psum(part_out.astype(jnp.bfloat16), "rep").astype(jnp.float32),
        lax.psum(part_gate.astype(jnp.bfloat16), "rep").astype(jnp.float32),
        lax.psum(part_up.astype(jnp.bfloat16), "rep").astype(jnp.float32),
        lax.psum(part_down.astype(jnp.bfloat16), "rep").astype(jnp.float32),
        lax.psum(part_gain_one.astype(jnp.bfloat16), "rep").astype(jnp.float32),
        lax.psum(part_bias_one.astype(jnp.bfloat16), "rep").astype(jnp.float32),
        lax.psum(part_gain_two.astype(jnp.bfloat16), "rep").astype(jnp.float32),
        lax.psum(part_bias_two.astype(jnp.bfloat16), "rep").astype(jnp.float32),
    )
    return (
        jnp.stack(outputs),
        jnp.stack(input_grads),
        totals[0],
        totals[1],
        totals[2],
        totals[3],
        totals[4],
        totals[5],
        totals[6],
        totals[7],
        totals[8],
    )


def solution(mesh):
    in_specs = (
        P(None, ("shard", "rep"), None),
        P(None, ("shard", "rep")),
        P("shard", None),
        P("shard", None),
        P("shard", None),
        P("shard", None),
        P("shard", None),
        P("shard"),
        P("shard"),
        P("shard"),
        P("shard"),
        P(None, ("shard", "rep"), None),
    )
    out_specs = (
        P(None, ("shard", "rep"), None),
        P(None, ("shard", "rep"), None),
        P("shard", None),
        P("shard", None),
        P("shard", None),
        P("shard", None),
        P("shard", None),
        P("shard"),
        P("shard"),
        P("shard"),
        P("shard"),
    )
    return jax.shard_map(shards, mesh=mesh, in_specs=in_specs, out_specs=out_specs, check_vma=False)
```

profile of v0, /device:TPU:0, one launch (start us, length us, event | category | flops | bytes accessed | tf_op | source)
XLA Modules:
  0.0 871.6 jit_solution(1877780145343959413)
XLA Ops:
  14.7 15.5 %all-reduce.9 = (bf16[768]{0:T(1024)(128)(2,1)S(1)}, bf16[768]{0:T(1024)(128)(2,1)S(1)}, bf16[768]{0:T(1024)(128)(2,1)S(1)}) all-reduce(bf16[768]{0:T(1024)(128)(2,1)S(1)} %dynamic-update-slice.1, bf16[768]{0:T(1024)(128)(2,1)S(1)} %dynamic-update-slice, ...), channel_id=1, replica_groups=mesh['shard'=8,'rep'=4] {'shard'}, use_global_device_ids=true, to_apply=%add.1 | all-reduce | flops 2304 | bytes 9216
  30.6 16.1 %all-gather.6.cloned.1.call-done = bf16[768,2304]{1,0:T(8,128)(2,1)} async-done(((bf16[96,2304]{1,0:T(8,128)(2,1)}), bf16[768,2304]{1,0:T(8,128)(2,1)}) %all-gather.6.cloned.1.call-update) | async-done | bytes 3538960 | tf_op jit(solution)/shard_map/all_gather | solution.py:270
  46.8 4.3 fusion.135
  61.8 3.0 copy.65
  64.8 3.2 copy.66
  70.5 2.8 fusion.132
  78.6 33.0 %while.57 = (s32[]{:T(128)}, bf16[12,512,64]{1,2,0:T(8,128)(2,1)S(1)}, f32[12,512]{1,0:T(8,128)S(1)}, bf16[12,512,64]{2,1,0:T(8,128)(2,1)S(1)}, bf16[12,512,64]{...) while((s32[]{:T(128)}, ...), condition=%wide.region_11.12_spmd.clone, body=%wide.region_8.11_spmd.clone.sunk | while | flops 69467648 | bytes 3696737 | solution.py:120
  111.7 3.0 copy.68
  119.1 34.3 %while.56 = (s32[]{:T(128)}, bf16[12,512,64]{1,2,0:T(8,128)(2,1)S(1)}, f32[12,512]{1,0:T(8,128)S(1)}, bf16[12,512,64]{2,1,0:T(8,128)(2,1)}, bf16[12,512,64]{2,1,...) while((s32[]{:T(128)}, ...), condition=%wide.region_3.4_spmd.clone, body=%wide.region_0.3_spmd.clone.sunk | while | flops 69467648 | bytes 3696737 | solution.py:120
  153.5 2.7 fusion.176
  161.6 7.5 fusion.180
  169.1 9.0 %multiply_convert_fusion.6 = (bf16[512,3072]{1,0:T(8,128)(2,1)}, f32[512,3072]{1,0:T(8,128)}) fusion(f32[512,3072]{1,0:T(8,128)} %fusion.180, bf16[512,768]{1,0:T(8,128)(2,1)S(1)} %get-tuple-element.540, bf16[768,3072]{1,0:T(8,128)(2,1)} %all-gather.12.cloned.1.call-done), kind=kOutput, calls=%fused_computation.120 | convolution fusion | flops 2425356288 | bytes 21233664 | tf_op jit(solution)/shard_map/dot_general | solution.py:13
  178.1 16.9 %all-gather.14.cloned.1.call-done = bf16[3072,768]{1,0:T(8,128)(2,1)} async-done(((bf16[384,768]{1,0:T(8,128)(2,1)}), bf16[3072,768]{1,0:T(8,128)(2,1)}) %all-gather.14.cloned.1.call-update) | async-done | bytes 4718608 | tf_op jit(solution)/shard_map/all_gather | solution.py:274
  195.0 6.1 fusion.178
  202.3 2.6 fusion.179
  204.9 5.0 multiply_convert_fusion.7
  210.0 2.8 fusion.177
  217.0 9.5 %multiply_convert_fusion.4 = (bf16[512,3072]{1,0:T(8,128)(2,1)}, bf16[512,3072]{1,0:T(8,128)(2,1)}) fusion(f32[512,3072]{1,0:T(8,128)S(1)} %fusion.179, f32[512,3072]{1,0:T(8,128)} %get-tuple-element.553, bf16[3072,768]{1,0:T(8,128)(2,1)} %all-gather.14.cloned.1.call-done, f32[512]{0:T(512)S(1)} %broadcast_multiply_fusion.6, ...), kind=kOutput, calls=%fused_computation.118 | convolution fusion | flops 2439905280 | bytes 25964544 | tf_op jit(solution)/shard_map/dot_general | solution.py:23
  226.5 4.8 fusion.181
  231.3 7.1 multiply_reduce_fusion.3
  238.4 9.8 %multiply_convert_fusion.2 = (bf16[512,3072]{1,0:T(8,128)(2,1)}, bf16[512,3072]{1,0:T(8,128)(2,1)}) fusion(f32[512,3072]{1,0:T(8,128)S(1)} %bitcast.388, f32[512,3072]{1,0:T(8,128)} %get-tuple-element.557, bf16[3072,768]{1,0:T(8,128)(2,1)} %all-gather.14.cloned.1.call-done, f32[512]{0:T(512)S(1)} %broadcast_multiply_fusion.2, ...), kind=kOutput, calls=%fused_computation.116 | convolution fusion | flops 2439905280 | bytes 25964544 | tf_op jit(solution)/shard_map/dot_general | solution.py:23
  248.3 4.8 fusion.182
  253.1 7.2 multiply_reduce_fusion.2
  263.2 2.3 copy.77
  268.2 99.7 %while.58 = (s32[]{:T(128)}, f32[12,512,64]{1,2,0:T(8,128)}, f32[12,512,64]{1,2,0:T(8,128)}, bf16[12,512,64]{1,2,0:T(8,128)(2,1)}, bf16[12,512,64]{2,1,0:T(8,128...) while((s32[]{:T(128)}, f32[12,512,64]{1,2,0:T(8,128)}, ...), condition=%wide.region_22.23_spmd.clone, body=%wide.region_20.22_spmd.clone.sunk | while | flops 170458624 | bytes 9063537 | solution.py:202
  374.6 92.3 %while.59 = (s32[]{:T(128)}, f32[12,512,64]{1,2,0:T(8,128)S(1)}, f32[12,512,64]{1,2,0:T(8,128)}, bf16[12,512,64]{1,2,0:T(8,128)(2,1)}, bf16[12,512,64]{2,1,0:T(8...) while((s32[]{:T(128)}, f32[12,512,64]{1,2,0:T(8,128)S(1)}, ...), condition=%wide.region_29.30_spmd.clone, body=%wide.region_27.29_spmd.clone.sunk | while | flops 170458624 | bytes 9063537 | solution.py:202
  466.9 3.1 multiply_bitcast_fusion.3
  472.9 2.9 fusion.119
  475.7 4.5 fusion.127
  480.3 5.1 fusion.92
  485.4 5.8 copy.88
  492.3 2.3 fusion.149
  496.8 6.0 fusion.152
  502.8 5.4 add_convert_fusion
  509.4 4.7 fusion.184
  514.1 4.6 add_convert_fusion.1
  519.1 4.7 fusion.183
  523.8 4.6 add_convert_fusion.2
  530.2 9.3 %reduce-scatter.16.cloned.1.call-done = bf16[96,2304]{1,0:T(8,128)(2,1)} async-done(((bf16[768,2304]{1,0:T(8,128)(2,1)}), bf16[96,2304]{1,0:T(8,128)(2,1)}) %reduce-scatter.16.cloned.1.call-update) | async-done | bytes 442384
  541.5 38.5 %reduce-scatter.8.cloned.1.call-done = bf16[96,768]{1,0:T(8,128)(2,1)} async-done(((bf16[768,768]{1,0:T(8,128)(2,1)}), bf16[96,768]{1,0:T(8,128)(2,1)}) %reduce-scatter.8.cloned.1.call-update) | async-done | bytes 147472 | tf_op jit(solution)/shard_map/reduce_scatter | solution.py:311
  580.0 57.8 %reduce-scatter.14.cloned.1.call-done = bf16[384,768]{1,0:T(8,128)(2,1)} async-done(((bf16[3072,768]{1,0:T(8,128)(2,1)}), bf16[384,768]{1,0:T(8,128)(2,1)}) %reduce-scatter.14.cloned.1.call-update) | async-done | bytes 589840 | tf_op jit(solution)/shard_map/reduce_scatter | solution.py:320
  637.8 57.4 %reduce-scatter.12.cloned.1.call-done = bf16[96,3072]{1,0:T(8,128)(2,1)} async-done(((bf16[768,3072]{1,0:T(8,128)(2,1)}), bf16[96,3072]{1,0:T(8,128)(2,1)}) %reduce-scatter.12.cloned.1.call-update) | async-done | bytes 589840 | tf_op jit(solution)/shard_map/reduce_scatter | solution.py:317
  695.2 57.6 %reduce-scatter.10.cloned.1.call-done = bf16[96,3072]{1,0:T(8,128)(2,1)} async-done(((bf16[768,3072]{1,0:T(8,128)(2,1)}), bf16[96,3072]{1,0:T(8,128)(2,1)}) %reduce-scatter.10.cloned.1.call-update) | async-done | bytes 589840 | tf_op jit(solution)/shard_map/reduce_scatter | solution.py:314
  752.9 23.9 %all-reduce.8 = (bf16[768]{0:T(1024)(128)(2,1)S(1)}, bf16[768]{0:T(1024)(128)(2,1)S(1)}, bf16[768]{0:T(1024)(128)(2,1)S(1)}, bf16[768]{0:T(1024)(128)(2,1)S(1)}, bf16[768]{0:T(1024)(128)(2,1)S(1)}) all-reduce(bf16[768]{0:T(1024)(128)(2,1)S(1)} %dynamic-update-slice.3, ...), channel_id=1, replica_groups=mesh['shard'=8,'rep'=4] {'shard'}, use_global_device_ids=true, to_apply=%add.3 | all-reduce | flops 3840 | bytes 15360
  777.1 12.4 %all-reduce.10 = (bf16[96]{0:T(256)(128)(2,1)S(1)}, bf16[96]{0:T(256)(128)(2,1)S(1)}, bf16[96]{0:T(256)(128)(2,1)S(1)}, bf16[96]{0:T(256)(128)(2,1)S(1)}) all-reduce(bf16[96]{0:T(256)(128)(2,1)S(1)} %dynamic-slice.5, bf16[96]{0:T(256)(128)(2,1)S(1)} %dynamic-slice.7, ...), channel_id=1, replica_groups=mesh['shard'=8,'rep'=4] {'rep'}, use_global_device_ids=true, to_apply=%region_43.44 | all-reduce | flops 384 | bytes 1536 | tf_op jit(solution)/shard_map/psum | solution.py:353
  791.5 4.9 fusion.125
  796.5 3.2 fusion.126
  803.5 54.9 %all-reduce.14.cloned.1.call-done = (bf16[96,2304]{0,1:T(8,128)(2,1)}, bf16[96,768]{1,0:T(8,128)(2,1)}, bf16[96,3072]{1,0:T(8,128)(2,1)}, bf16[96,3072]{1,0:T(8,128)(2,1)}, bf16[384,768]{1,0:T(8,128)(2,1)}) async-done(((bf16[96,2304]{0,1:T(8,128)(2,1)}, bf16[96,768]{1,0:T(8,128)(2,1)}, bf16[96,3072]{1,0:T(8,128)(2,1)}, bf16[96,3072]{1,0:T(8,128)(2,1)}, bf16[384,768]{1,0:T(8,128)(2,1)}), ...) | async-done | bytes 2359312 | tf_op jit(solution)/shard_map/psum | solution.py:348
  (574 shorter events, 333.0 us)
Async XLA Ops:
  7.2 39.6 %all-gather.6.cloned.1.call-start = ((), (), s32[]{:S(2)}) async-start(), calls=%async_computation.5 | async-start | bytes 3981312 | tf_op jit(solution)/shard_map/all_gather | solution.py:270
  7.9 145.5 %all-gather.8.cloned.1.call-start = ((), (), s32[]{:S(2)}) async-start(), calls=%async_computation.6 | async-start | bytes 1327104 | tf_op jit(solution)/shard_map/all_gather | solution.py:271
  8.7 152.9 %all-gather.10.cloned.1.call-start = ((), (), s32[]{:S(2)}) async-start(), calls=%async_computation.7 | async-start | bytes 5308416 | tf_op jit(solution)/shard_map/all_gather | solution.py:272
  9.4 159.7 %all-gather.12.cloned.1.call-start = ((), (), s32[]{:S(2)}) async-start(), calls=%async_computation.8 | async-start | bytes 5308416 | tf_op jit(solution)/shard_map/all_gather | solution.py:273
  10.0 185.0 %all-gather.14.cloned.1.call-start = ((), (), s32[]{:S(2)}) async-start(), calls=%async_computation.9 | async-start | bytes 5308416 | tf_op jit(solution)/shard_map/all_gather | solution.py:274
  10.6 528.9 %reduce-scatter.16.cloned.1.call-start = ((), (), s32[]{:S(2)}) async-start(), calls=%async_computation.14 | async-start | bytes 3981312
  30.6 39.9 %copy-start.38 = (f32[512,64]{0,1:T(8,128)}, f32[512,64]{0,1:T(8,128)S(1)}, u32[]{:S(2)}) copy-start(f32[512,64]{0,1:T(8,128)S(1)} %get-tuple-element.562) | copy-start | bytes 393220
  30.6 39.9 %copy-start.40 = (f32[512,64]{0,1:T(8,128)}, f32[512,64]{0,1:T(8,128)S(1)}, u32[]{:S(2)}) copy-start(f32[512,64]{0,1:T(8,128)S(1)} %get-tuple-element.563) | copy-start | bytes 393220
  111.6 4.5 copy-start.4
  111.6 4.5 copy-start.29
  119.1 34.3 %copy-start.5 = (bf16[12,512,64]{1,2,0:T(8,128)(2,1)S(1)}, bf16[12,512,64]{1,2,0:T(8,128)(2,1)}, u32[]{:S(2)}) copy-start(bf16[12,512,64]{1,2,0:T(8,128)(2,1)} %copy-done.4) | copy-start | bytes 2359300
  161.6 7.5 copy-start.32
  169.1 25.9 %copy-start.11 = (f32[512,768]{1,0:T(8,128)S(1)}, f32[512,768]{1,0:T(8,128)}, u32[]{:S(2)}) copy-start(f32[512,768]{1,0:T(8,128)} %copy-done.10) | copy-start | bytes 4718596
  195.0 6.5 slice-start
  195.0 6.5 slice-start.1
  202.3 7.7 slice-start.6
  204.9 5.1 copy-start.23
  204.9 5.1 slice-start.7
  212.8 18.5 %copy-start.8 = (f32[512,768]{1,0:T(8,128)}, f32[512,768]{1,0:T(8,128)S(1)}, u32[]{:S(2)}) copy-start(f32[512,768]{1,0:T(8,128)S(1)} %get-tuple-element.555) | copy-start | bytes 4718596
  226.5 4.8 copy-start.24
  226.5 4.8 copy-start.35
  226.5 11.9 %slice-start.2 = ((s8[6291456]{0:T(1024)(128)(4,1)}), s8[4194304]{0:T(1024)(128)(4,1)S(1)}, s32[]{:S(2)}) async-start(s8[6291456]{0:T(1024)(128)(4,1)} %bitcast.387), calls=%async_computation.18 | async-start | bytes 8388608
  231.3 7.1 slice-start.3
  248.2 4.8 copy-start.25
  248.2 4.8 copy-start.68
  248.2 4.8 copy-start.71
  253.1 8.5 copy-start.60
  374.6 92.3 %copy-start.41 = (f32[512,64]{0,1:T(8,128)S(1)}, f32[512,64]{0,1:T(8,128)}, u32[]{:S(2)}) copy-start(f32[512,64]{0,1:T(8,128)} %copy-done.40) | copy-start | bytes 393220
  475.7 4.5 copy-start.42
  475.7 4.5 copy-start.44
  475.7 4.6 copy-start.58
  491.3 88.8 %reduce-scatter.8.cloned.1.call-start = ((), (), s32[]{:S(2)}) async-start(), calls=%async_computation.10 | async-start | bytes 1327104 | tf_op jit(solution)/shard_map/reduce_scatter | solution.py:311
  496.5 6.3 copy-start.20
  496.5 141.3 %reduce-scatter.14.cloned.1.call-start = ((), (), s32[]{:S(2)}) async-start(), calls=%async_computation.13 | async-start | bytes 5308416 | tf_op jit(solution)/shard_map/reduce_scatter | solution.py:320
  496.8 6.1 copy-start.70
  508.2 5.9 copy-start.33
  508.3 186.9 %reduce-scatter.12.cloned.1.call-start = ((), (), s32[]{:S(2)}) async-start(), calls=%async_computation.12 | async-start | bytes 5308416 | tf_op jit(solution)/shard_map/reduce_scatter | solution.py:317
  509.4 4.8 copy-start.69
  518.8 234.0 %reduce-scatter.10.cloned.1.call-start = ((), (), s32[]{:S(2)}) async-start(), calls=%async_computation.11 | async-start | bytes 5308416 | tf_op jit(solution)/shard_map/reduce_scatter | solution.py:314
  519.0 4.8 copy-start.67
  528.4 330.1 %all-reduce.14.cloned.1.call-start = ((), (), s32[]{:S(2)}) async-start(), calls=%async_computation.15 | async-start | bytes 5013504 | tf_op jit(solution)/shard_map/psum | solution.py:348
  530.1 222.7 %copy-start.50 = (f32[768]{0:T(1024)S(1)}, f32[768]{0:T(1024)}, u32[]{:S(2)}) copy-start(f32[768]{0:T(1024)} %get-tuple-element.388) | copy-start | bytes 9220
  530.1 222.7 %copy-start.51 = (f32[768]{0:T(1024)S(1)}, f32[768]{0:T(1024)}, u32[]{:S(2)}) copy-start(f32[768]{0:T(1024)} %get-tuple-element.397) | copy-start | bytes 9220
  530.1 261.4 %copy-start.37 = (f32[512,768]{1,0:T(8,128)S(1)}, f32[512,768]{1,0:T(8,128)}, u32[]{:S(2)}) copy-start(f32[512,768]{1,0:T(8,128)} %copy-done.36) | copy-start | bytes 4718596
  791.5 4.9 copy-start.28
  791.5 4.9 copy-start.43
  791.5 5.0 copy-start.45
  791.5 5.0 copy-start.55
  (43 other events, 92.1 us)
Sparse Core Ops, SparseCore 0:
  9.9 36.8 all-gather.5
  48.7 24.0 all-gather.7
  74.6 38.9 all-gather.9
  115.3 38.9 all-gather.11
  156.0 38.9 all-gather.13
  491.4 48.0 reduce-scatter.15
  543.3 36.7 reduce-scatter.7
  583.9 53.8 reduce-scatter.13
  641.3 53.8 reduce-scatter.11
  698.9 53.9 reduce-scatter.9
  756.2 102.2 all-reduce.13
where the time goes:
time: 885 us; the launch traced here: 872 us
  matrix products  385 us (44%)
  waiting for transfers between devices  312 us (35%)
  local copies, waits for them, and re-layouts  64 us (7%)
  blocking collectives  51.8 us (6%)
  other arithmetic  39.6 us (4%)
  between operations  16.6 us (2%)
    dot_general x82, matrix products, times_transposed(): lax.dot_general(left_op, right_op, (((1,), (1,)), ((), ())), preferred_el...  147 us
    dot_general x58, matrix products, inner_sum(): lax.dot_general(left_op, right_op, (((0,), (0,)), ((), ())), preferred_el...  130 us
    dot_general x58, matrix products, matmul(): return jnp.dot(left_op, right_op, preferred_element_type=jnp.float32)  108 us
    reduce_scatter x1, waiting for transfers between devices, shards(): lax.psum_scatter(sum_down.astype(jnp.bfloat16), 'shard', scatter_dimensio...  57.8 us
    reduce_scatter x1, waiting for transfers between devices, shards(): lax.psum_scatter(sum_gate.astype(jnp.bfloat16), 'shard', scatter_dimensio...  57.6 us
    reduce_scatter x1, waiting for transfers between devices, shards(): lax.psum_scatter(sum_up.astype(jnp.bfloat16), 'shard', scatter_dimension=...  57.4 us
    psum x1, waiting for transfers between devices, shards(): lax.psum(part_qkv.astype(jnp.bfloat16), 'rep').astype(jnp.float32)  54.9 us
    unnamed x2, blocking collectives  39.4 us
  transfers between devices with their start and end apart: 11, of which 8 were waited for; matrix products, arithmetic and copies ran while one was open for 20% of the time, Pallas kernels for 0%

commit v1 on v0

--- a/solution.py
+++ b/solution.py
@@ -345,7 +345,7 @@
         part_bias_two,
     ) = summed
     totals = (
-        lax.psum(part_qkv.astype(jnp.bfloat16), "rep").astype(jnp.float32),
+        jax.lax.all_gather(part_qkv.astype(jnp.bfloat16), "rep").sum(axis=0).astype(jnp.float32),
         lax.psum(part_out.astype(jnp.bfloat16), "rep").astype(jnp.float32),
         lax.psum(part_gate.astype(jnp.bfloat16), "rep").astype(jnp.float32),
         lax.psum(part_up.astype(jnp.bfloat16), "rep").astype(jnp.float32),

time: 885 us -> 903 us (1.020)
  waiting for transfers between devices: 312 us -> 332 us
    psum x1, waiting for transfers between devices: 54.9 us -> 72.3 us  [shards(): lax.psum(part_out.astype(jnp.bfloat16), 'rep').astype(jnp.float32)]
    reduce_scatter x0 -> x1, waiting for transfers between devices: none -> 11.1 us  [shards(): lax.psum_scatter(sum_qkv.astype(jnp.bfloat16), 'shard', scatter_dimension...]
    unnamed x12, waiting for transfers between devices: 12.5 us -> 3.23 us
    unnamed x184 -> x180, local copies, waits for them, and re-layouts: 39.2 us -> 35.4 us
  transfers between devices with their start and end apart: 11 -> 12, of which waited for: 8 -> 8; matrix products, arithmetic and copies ran while one was open for 20% -> 20% of each run, Pallas kernels for 0% -> 0%
where the time goes in v1:
time: 903 us; the launch traced here: 890 us
  matrix products  384 us (43%)
  waiting for transfers between devices  332 us (37%)
  local copies, waits for them, and re-layouts  60.3 us (7%)
  blocking collectives  51.4 us (6%)
  other arithmetic  42.4 us (5%)
  between operations  16.9 us (2%)
    dot_general x82, matrix products, times_transposed(): lax.dot_general(left_op, right_op, (((1,), (1,)), ((), ())), preferred_el...  147 us
    dot_general x58, matrix products, inner_sum(): lax.dot_general(left_op, right_op, (((0,), (0,)), ((), ())), preferred_el...  130 us
    dot_general x58, matrix products, matmul(): return jnp.dot(left_op, right_op, preferred_element_type=jnp.float32)  108 us
    psum x1, waiting for transfers between devices, shards(): lax.psum(part_out.astype(jnp.bfloat16), 'rep').astype(jnp.float32)  72.3 us
    reduce_scatter x1, waiting for transfers between devices, shards(): lax.psum_scatter(sum_down.astype(jnp.bfloat16), 'shard', scatter_dimensio...  57.8 us
    reduce_scatter x1, waiting for transfers between devices, shards(): lax.psum_scatter(sum_gate.astype(jnp.bfloat16), 'shard', scatter_dimensio...  57.6 us
    reduce_scatter x1, waiting for transfers between devices, shards(): lax.psum_scatter(sum_up.astype(jnp.bfloat16), 'shard', scatter_dimension=...  57.4 us
    unnamed x2, blocking collectives  39.4 us
  transfers between devices with their start and end apart: 12, of which 8 were waited for; matrix products, arithmetic and copies ran while one was open for 20% of the time, Pallas kernels for 0%

profile of v1, /device:TPU:0, one launch (start us, length us, event | category | flops | bytes accessed | tf_op | source)
XLA Modules:
  0.0 890.1 jit_solution(7933489836990425746)
XLA Ops:
  14.7 15.5 %all-reduce.9 = (bf16[768]{0:T(1024)(128)(2,1)S(1)}, bf16[768]{0:T(1024)(128)(2,1)S(1)}, bf16[768]{0:T(1024)(128)(2,1)S(1)}) all-reduce(bf16[768]{0:T(1024)(128)(2,1)S(1)} %dynamic-update-slice.1, bf16[768]{0:T(1024)(128)(2,1)S(1)} %dynamic-update-slice, ...), channel_id=1, replica_groups=mesh['shard'=8,'rep'=4] {'shard'}, use_global_device_ids=true, to_apply=%add.1 | all-reduce | flops 2304 | bytes 9216
  30.6 16.1 %all-gather.8.cloned.1.call-done = bf16[768,2304]{1,0:T(8,128)(2,1)} async-done(((bf16[96,2304]{1,0:T(8,128)(2,1)}), bf16[768,2304]{1,0:T(8,128)(2,1)}) %all-gather.8.cloned.1.call-update) | async-done | bytes 3538960 | tf_op jit(solution)/shard_map/all_gather | solution.py:270
  46.8 4.3 fusion.135
  61.8 3.0 copy.64
  64.8 3.2 copy.65
  70.5 2.8 fusion.132
  78.6 33.1 %while.57 = (s32[]{:T(128)}, bf16[12,512,64]{1,2,0:T(8,128)(2,1)S(1)}, f32[12,512]{1,0:T(8,128)S(1)}, bf16[12,512,64]{2,1,0:T(8,128)(2,1)S(1)}, bf16[12,512,64]{...) while((s32[]{:T(128)}, ...), condition=%wide.region_11.12_spmd.clone, body=%wide.region_8.11_spmd.clone.sunk | while | flops 69467648 | bytes 3696737 | solution.py:120
  111.7 3.0 copy.67
  119.2 34.3 %while.56 = (s32[]{:T(128)}, bf16[12,512,64]{1,2,0:T(8,128)(2,1)S(1)}, f32[12,512]{1,0:T(8,128)S(1)}, bf16[12,512,64]{2,1,0:T(8,128)(2,1)}, bf16[12,512,64]{2,1,...) while((s32[]{:T(128)}, ...), condition=%wide.region_3.4_spmd.clone, body=%wide.region_0.3_spmd.clone.sunk | while | flops 69467648 | bytes 3696737 | solution.py:120
  153.5 2.7 fusion.176
  161.7 7.4 fusion.180
  169.1 9.0 %multiply_convert_fusion.6 = (bf16[512,3072]{1,0:T(8,128)(2,1)}, f32[512,3072]{1,0:T(8,128)}) fusion(f32[512,3072]{1,0:T(8,128)} %fusion.180, bf16[512,768]{1,0:T(8,128)(2,1)S(1)} %get-tuple-element.506, bf16[768,3072]{1,0:T(8,128)(2,1)} %all-gather.14.cloned.1.call-done), kind=kOutput, calls=%fused_computation.120 | convolution fusion | flops 2425356288 | bytes 21233664 | tf_op jit(solution)/shard_map/dot_general | solution.py:13
  178.1 16.9 %all-gather.16.cloned.1.call-done = bf16[3072,768]{1,0:T(8,128)(2,1)} async-done(((bf16[384,768]{1,0:T(8,128)(2,1)}), bf16[3072,768]{1,0:T(8,128)(2,1)}) %all-gather.16.cloned.1.call-update) | async-done | bytes 4718608 | tf_op jit(solution)/shard_map/all_gather | solution.py:274
  195.0 6.1 fusion.178
  202.3 2.6 fusion.179
  204.9 5.0 multiply_convert_fusion.7
  210.0 2.8 fusion.177
  217.0 9.5 %multiply_convert_fusion.4 = (bf16[512,3072]{1,0:T(8,128)(2,1)}, bf16[512,3072]{1,0:T(8,128)(2,1)}) fusion(f32[512,3072]{1,0:T(8,128)S(1)} %fusion.179, f32[512,3072]{1,0:T(8,128)} %get-tuple-element.519, bf16[3072,768]{1,0:T(8,128)(2,1)} %all-gather.16.cloned.1.call-done, f32[512]{0:T(512)S(1)} %broadcast_multiply_fusion.6, ...), kind=kOutput, calls=%fused_computation.118 | convolution fusion | flops 2439905280 | bytes 25964544 | tf_op jit(solution)/shard_map/dot_general | solution.py:23
  226.5 4.8 fusion.181
  231.3 7.1 multiply_reduce_fusion.3
  238.4 9.8 %multiply_convert_fusion.2 = (bf16[512,3072]{1,0:T(8,128)(2,1)}, bf16[512,3072]{1,0:T(8,128)(2,1)}) fusion(f32[512,3072]{1,0:T(8,128)S(1)} %bitcast.389, f32[512,3072]{1,0:T(8,128)} %get-tuple-element.523, bf16[3072,768]{1,0:T(8,128)(2,1)} %all-gather.16.cloned.1.call-done, f32[512]{0:T(512)S(1)} %broadcast_multiply_fusion.2, ...), kind=kOutput, calls=%fused_computation.116 | convolution fusion | flops 2439905280 | bytes 25964544 | tf_op jit(solution)/shard_map/dot_general | solution.py:23
  248.2 4.8 fusion.182
  253.1 7.2 multiply_reduce_fusion.2
  263.2 2.3 copy.76
  268.2 99.5 %while.58 = (s32[]{:T(128)}, f32[12,512,64]{1,2,0:T(8,128)}, f32[12,512,64]{1,2,0:T(8,128)}, bf16[12,512,64]{1,2,0:T(8,128)(2,1)}, bf16[12,512,64]{2,1,0:T(8,128...) while((s32[]{:T(128)}, f32[12,512,64]{1,2,0:T(8,128)}, ...), condition=%wide.region_22.23_spmd.clone, body=%wide.region_20.22_spmd.clone.sunk | while | flops 170458624 | bytes 9063537 | solution.py:202
  374.3 92.2 %while.59 = (s32[]{:T(128)}, f32[12,512,64]{1,2,0:T(8,128)S(1)}, f32[12,512,64]{1,2,0:T(8,128)}, bf16[12,512,64]{1,2,0:T(8,128)(2,1)}, bf16[12,512,64]{2,1,0:T(8...) while((s32[]{:T(128)}, f32[12,512,64]{1,2,0:T(8,128)S(1)}, ...), condition=%wide.region_29.30_spmd.clone, body=%wide.region_27.29_spmd.clone.sunk | while | flops 170458624 | bytes 9063537 | solution.py:202
  466.5 3.1 multiply_bitcast_fusion.3
  472.5 2.9 fusion.119
  475.4 4.5 fusion.127
  480.0 5.1 fusion.92
  485.1 5.8 copy.87
  492.0 2.3 fusion.149
  496.4 6.0 fusion.152
  502.5 5.4 add_convert_fusion
  509.0 4.7 fusion.184
  513.8 4.6 add_convert_fusion.1
  518.6 4.7 fusion.183
  523.4 4.6 add_convert_fusion.2
  528.1 11.1 %reduce-scatter.16.cloned.1.call-done = bf16[96,2304]{1,0:T(8,128)(2,1)} async-done(((bf16[768,2304]{1,0:T(8,128)(2,1)}), bf16[96,2304]{1,0:T(8,128)(2,1)}) %reduce-scatter.16.cloned.1.call-update) | async-done | bytes 442384 | tf_op jit(solution)/shard_map/reduce_scatter | solution.py:308
  540.5 39.3 %reduce-scatter.8.cloned.1.call-done = bf16[96,768]{1,0:T(8,128)(2,1)} async-done(((bf16[768,768]{1,0:T(8,128)(2,1)}), bf16[96,768]{1,0:T(8,128)(2,1)}) %reduce-scatter.8.cloned.1.call-update) | async-done | bytes 147472 | tf_op jit(solution)/shard_map/reduce_scatter | solution.py:311
  579.7 57.8 %reduce-scatter.14.cloned.1.call-done = bf16[384,768]{1,0:T(8,128)(2,1)} async-done(((bf16[3072,768]{1,0:T(8,128)(2,1)}), bf16[384,768]{1,0:T(8,128)(2,1)}) %reduce-scatter.14.cloned.1.call-update) | async-done | bytes 589840 | tf_op jit(solution)/shard_map/reduce_scatter | solution.py:320
  637.5 57.4 %reduce-scatter.12.cloned.1.call-done = bf16[96,3072]{1,0:T(8,128)(2,1)} async-done(((bf16[768,3072]{1,0:T(8,128)(2,1)}), bf16[96,3072]{1,0:T(8,128)(2,1)}) %reduce-scatter.12.cloned.1.call-update) | async-done | bytes 589840 | tf_op jit(solution)/shard_map/reduce_scatter | solution.py:317
  694.9 57.6 %reduce-scatter.10.cloned.1.call-done = bf16[96,3072]{1,0:T(8,128)(2,1)} async-done(((bf16[768,3072]{1,0:T(8,128)(2,1)}), bf16[96,3072]{1,0:T(8,128)(2,1)}) %reduce-scatter.10.cloned.1.call-update) | async-done | bytes 589840 | tf_op jit(solution)/shard_map/reduce_scatter | solution.py:314
  752.5 23.9 %all-reduce.8 = (bf16[768]{0:T(1024)(128)(2,1)S(1)}, bf16[768]{0:T(1024)(128)(2,1)S(1)}, bf16[768]{0:T(1024)(128)(2,1)S(1)}, bf16[768]{0:T(1024)(128)(2,1)S(1)}, bf16[768]{0:T(1024)(128)(2,1)S(1)}) all-reduce(bf16[768]{0:T(1024)(128)(2,1)S(1)} %dynamic-update-slice.3, ...), channel_id=1, replica_groups=mesh['shard'=8,'rep'=4] {'shard'}, use_global_device_ids=true, to_apply=%add.3 | all-reduce | flops 3840 | bytes 15360
  776.7 12.0 %all-reduce.10 = (bf16[96]{0:T(256)(128)(2,1)S(1)}, bf16[96]{0:T(256)(128)(2,1)S(1)}, bf16[96]{0:T(256)(128)(2,1)S(1)}, bf16[96]{0:T(256)(128)(2,1)S(1)}) all-reduce(bf16[96]{0:T(256)(128)(2,1)S(1)} %dynamic-slice.5, bf16[96]{0:T(256)(128)(2,1)S(1)} %dynamic-slice.7, ...), channel_id=1, replica_groups=mesh['shard'=8,'rep'=4] {'rep'}, use_global_device_ids=true, to_apply=%region_43.44 | all-reduce | flops 384 | bytes 1536 | tf_op jit(solution)/shard_map/psum | solution.py:353
  790.8 4.9 fusion.125
  795.8 3.2 fusion.126
  805.5 72.3 %all-reduce.14.cloned.1.call-done = (bf16[96,768]{1,0:T(8,128)(2,1)}, bf16[96,3072]{1,0:T(8,128)(2,1)}, bf16[96,3072]{1,0:T(8,128)(2,1)}, bf16[384,768]{1,0:T(8,128)(2,1)}) async-done(((bf16[96,768]{1,0:T(8,128)(2,1)}, bf16[96,3072]{1,0:T(8,128)(2,1)}, bf16[96,3072]{1,0:T(8,128)(2,1)}, bf16[384,768]{1,0:T(8,128)(2,1)}), (bf16[96,768]{1,0:T(8,128)(2,1)}, bf16[96,3072]{1,0:T(8,128)(2,1)}, ...) | async-done | bytes 1916944 | tf_op jit(solution)/shard_map/psum | solution.py:349
  (575 shorter events, 331.8 us)
Async XLA Ops:
  7.2 39.6 %all-gather.8.cloned.1.call-start = ((), (), s32[]{:S(2)}) async-start(), calls=%async_computation.5 | async-start | bytes 3981312 | tf_op jit(solution)/shard_map/all_gather | solution.py:270
  7.9 145.6 %all-gather.10.cloned.1.call-start = ((), (), s32[]{:S(2)}) async-start(), calls=%async_computation.6 | async-start | bytes 1327104 | tf_op jit(solution)/shard_map/all_gather | solution.py:271
  8.7 153.0 %all-gather.12.cloned.1.call-start = ((), (), s32[]{:S(2)}) async-start(), calls=%async_computation.7 | async-start | bytes 5308416 | tf_op jit(solution)/shard_map/all_gather | solution.py:272
  9.4 159.7 %all-gather.14.cloned.1.call-start = ((), (), s32[]{:S(2)}) async-start(), calls=%async_computation.8 | async-start | bytes 5308416 | tf_op jit(solution)/shard_map/all_gather | solution.py:273
  10.0 185.0 %all-gather.16.cloned.1.call-start = ((), (), s32[]{:S(2)}) async-start(), calls=%async_computation.9 | async-start | bytes 5308416 | tf_op jit(solution)/shard_map/all_gather | solution.py:274
  10.6 528.6 %reduce-scatter.16.cloned.1.call-start = ((), (), s32[]{:S(2)}) async-start(), calls=%async_computation.15 | async-start | bytes 3981312 | tf_op jit(solution)/shard_map/reduce_scatter | solution.py:308
  30.6 39.9 %copy-start.38 = (f32[512,64]{0,1:T(8,128)}, f32[512,64]{0,1:T(8,128)S(1)}, u32[]{:S(2)}) copy-start(f32[512,64]{0,1:T(8,128)S(1)} %get-tuple-element.528) | copy-start | bytes 393220
  30.6 39.9 %copy-start.40 = (f32[512,64]{0,1:T(8,128)}, f32[512,64]{0,1:T(8,128)S(1)}, u32[]{:S(2)}) copy-start(f32[512,64]{0,1:T(8,128)S(1)} %get-tuple-element.529) | copy-start | bytes 393220
  119.2 34.3 %copy-start.5 = (bf16[12,512,64]{1,2,0:T(8,128)(2,1)S(1)}, bf16[12,512,64]{1,2,0:T(8,128)(2,1)}, u32[]{:S(2)}) copy-start(bf16[12,512,64]{1,2,0:T(8,128)(2,1)} %copy-done.4) | copy-start | bytes 2359300
  161.7 7.4 copy-start.32
  169.1 25.9 %copy-start.11 = (f32[512,768]{1,0:T(8,128)S(1)}, f32[512,768]{1,0:T(8,128)}, u32[]{:S(2)}) copy-start(f32[512,768]{1,0:T(8,128)} %copy-done.10) | copy-start | bytes 4718596
  195.0 6.5 slice-start
  195.0 6.5 slice-start.1
  202.3 7.7 slice-start.6
  204.9 5.0 copy-start.23
  204.9 5.0 slice-start.7
  212.8 18.5 %copy-start.8 = (f32[512,768]{1,0:T(8,128)}, f32[512,768]{1,0:T(8,128)S(1)}, u32[]{:S(2)}) copy-start(f32[512,768]{1,0:T(8,128)S(1)} %get-tuple-element.521) | copy-start | bytes 4718596
  226.5 4.8 copy-start.24
  226.5 4.8 copy-start.35
  226.5 11.9 %slice-start.2 = ((s8[6291456]{0:T(1024)(128)(4,1)}), s8[4194304]{0:T(1024)(128)(4,1)S(1)}, s32[]{:S(2)}) async-start(s8[6291456]{0:T(1024)(128)(4,1)} %bitcast.388), calls=%async_computation.19 | async-start | bytes 8388608
  231.3 7.1 slice-start.3
  248.2 4.8 copy-start.25
  248.2 4.8 copy-start.67
  248.2 4.8 copy-start.70
  253.1 8.5 copy-start.59
  374.3 92.2 %copy-start.41 = (f32[512,64]{0,1:T(8,128)S(1)}, f32[512,64]{0,1:T(8,128)}, u32[]{:S(2)}) copy-start(f32[512,64]{0,1:T(8,128)} %copy-done.40) | copy-start | bytes 393220
  475.4 4.5 copy-start.44
  475.4 4.6 copy-start.57
  490.9 88.8 %reduce-scatter.8.cloned.1.call-start = ((), (), s32[]{:S(2)}) async-start(), calls=%async_computation.10 | async-start | bytes 1327104 | tf_op jit(solution)/shard_map/reduce_scatter | solution.py:311
  496.2 6.3 copy-start.20
  496.2 141.3 %reduce-scatter.14.cloned.1.call-start = ((), (), s32[]{:S(2)}) async-start(), calls=%async_computation.13 | async-start | bytes 5308416 | tf_op jit(solution)/shard_map/reduce_scatter | solution.py:320
  496.4 6.1 copy-start.69
  507.9 5.9 copy-start.33
  507.9 187.0 %reduce-scatter.12.cloned.1.call-start = ((), (), s32[]{:S(2)}) async-start(), calls=%async_computation.12 | async-start | bytes 5308416 | tf_op jit(solution)/shard_map/reduce_scatter | solution.py:317
  509.0 4.8 copy-start.68
  518.4 234.1 %reduce-scatter.10.cloned.1.call-start = ((), (), s32[]{:S(2)}) async-start(), calls=%async_computation.11 | async-start | bytes 5308416 | tf_op jit(solution)/shard_map/reduce_scatter | solution.py:314
  518.6 4.8 copy-start.66
  528.0 11.3 %copy-start.64 = (bf16[96]{0:T(256)(128)(2,1)S(1)}, bf16[96]{0:T(256)(128)(2,1)}, u32[]{:S(2)}) copy-start(bf16[96]{0:T(256)(128)(2,1)} %param.30) | copy-start | bytes 580
  528.0 12.2 %copy-start.21 = (bf16[2,512,768]{2,1,0:T(8,128)(2,1)S(1)}, bf16[2,512,768]{2,1,0:T(8,128)(2,1)}, u32[]{:S(2)}) copy-start(bf16[2,512,768]{2,1,0:T(8,128)(2,1)} %param.31) | copy-start | bytes 4718596
  528.0 12.4 %copy-start.49 = (f32[768]{0:T(1024)S(1)}, f32[768]{0:T(1024)}, u32[]{:S(2)}) copy-start(f32[768]{0:T(1024)} %get-tuple-element.355) | copy-start | bytes 9220
  528.0 12.4 %copy-start.50 = (f32[768]{0:T(1024)S(1)}, f32[768]{0:T(1024)}, u32[]{:S(2)}) copy-start(f32[768]{0:T(1024)} %get-tuple-element.364) | copy-start | bytes 9220
  528.0 274.8 %all-gather.18.cloned.1.call-start = ((), (), s32[]{:S(2)}) async-start(), calls=%async_computation.14 | async-start | bytes 2211840 | tf_op jit(solution)/shard_map/all_gather | solution.py:348
  539.2 338.6 %all-reduce.14.cloned.1.call-start = ((), (), s32[]{:S(2)}) async-start(), calls=%async_computation.16 | async-start | bytes 3833856 | tf_op jit(solution)/shard_map/psum | solution.py:349
  540.4 250.4 %copy-start.37 = (f32[512,768]{1,0:T(8,128)S(1)}, f32[512,768]{1,0:T(8,128)}, u32[]{:S(2)}) copy-start(f32[512,768]{1,0:T(8,128)} %copy-done.36) | copy-start | bytes 4718596
  790.8 4.9 copy-start.28
  790.8 4.9 copy-start.43
  790.8 4.9 copy-start.45
  790.8 4.9 copy-start.54
  (43 other events, 101.2 us)
Sparse Core Ops, SparseCore 0:
  9.9 36.8 all-gather.7
  48.7 24.0 all-gather.9
  74.6 38.9 all-gather.11
  115.3 38.9 all-gather.13
  156.1 38.8 all-gather.15
  491.0 48.0 reduce-scatter.15
  543.0 36.7 reduce-scatter.7
  583.6 53.8 reduce-scatter.13
  641.0 53.8 reduce-scatter.11
  698.5 53.8 reduce-scatter.9
  754.1 40.5 all-gather.17
  797.1 80.5 all-reduce.13
